TPU v7x, 128 devices: a whole 4x4x4 slice. The times are simulated.
128 devices in a mesh: section: 4 (over x), dp: 8 (over z_lo, y), tensor: 4 (over z_hi, core).
Axes of the slice: x: 4, y: 4, z: 4 (z_hi: 2, z_lo: 2; z = z_hi * 2 + z_lo), core: 2. Of those that a mesh axis runs over, the one named last changes fastest.
Arguments:
- saved: bfloat16 [4, 4096, 5120], P('section', ('dp', 'tensor')), may hold values from -0.09375 to 0.09375
- weight: bfloat16 [4, 5120, 5120], P('section', None, 'tensor'), may hold values from -0.078125 to 0.078125
- out_grad: bfloat16 [4096, 5120], P(('dp', 'tensor')), may hold values from -6 to 6
Outputs:
- input_grads: bfloat16 [4, 4096, 5120], P('section', ('dp', 'tensor'))
- weight_grads: float32 [4, 5120, 5120], P('section', 'dp', 'tensor')
All inputs are finite; a program needn't handle non-finite values.
Results may differ from a plain program's by a relative error of at most 0.02.
Values may be sent and summed in bfloat16 or wider, within the bound.
A program may use at most 192 MiB of HBM per device.

v0:
```python
import jax
import jax.numpy as jnp
from jax import lax
from jax.sharding import PartitionSpec as P


def from_behind(block, axis, distance):
    devices = range(lax.axis_size(axis))
    route = [(i - distance, i) for i in devices if i - distance in devices]
    return lax.ppermute(block, axis, route)


def on_device(saved, weight, out_grad):
    activations = saved[0]
    weight_cols = weight[0]
    sections = lax.axis_size("section")
    section_index = lax.axis_index("section")
    gradient = out_grad
    own_input = jnp.zeros(out_grad.shape, jnp.bfloat16)
    kept_columns = jnp.zeros(
        (out_grad.shape[0] * lax.axis_size("tensor"), weight_cols.shape[1]), jnp.bfloat16
    )
    for rounds in range(sections):
        active = sections - 1 - rounds
        on_duty = section_index == active
        columns = lax.all_to_all(gradient, "tensor", split_axis=1, concat_axis=0, tiled=True)

        def compute(operand):
            return lax.dot_general(
                operand, weight_cols, (((1,), (1,)), ((), ())), preferred_element_type=jnp.float32
            )

        def nothing(operand):
            return jnp.zeros((operand.shape[0], weight_cols.shape[0]), jnp.float32)

        returned = lax.psum_scatter(
            lax.cond(on_duty, compute, nothing, columns).astype(jnp.bfloat16),
            "tensor",
            scatter_dimension=0,
            tiled=True,
        ).astype(jnp.float32)
        updated = (gradient.astype(jnp.float32) + returned).astype(jnp.bfloat16)
        own_input = jnp.where(on_duty, updated, own_input)
        kept_columns = jnp.where(on_duty, columns, kept_columns)
        if rounds + 1 < sections:
            gradient = from_behind(updated, "section", -1)
    gathered = lax.all_gather(activations, "tensor", axis=0, tiled=True)
    weight_grad = lax.psum_scatter(
        lax.dot_general(
            gathered, kept_columns, (((0,), (0,)), ((), ())), preferred_element_type=jnp.float32
        ).astype(jnp.bfloat16),
        "dp",
        scatter_dimension=0,
        tiled=True,
    ).astype(jnp.float32)
    return (own_input[None], weight_grad[None])


def solution(mesh):
    placed = (
        P("section", ("dp", "tensor"), None),
        P("section", None, "tensor"),
        P(("dp", "tensor"), None),
    )
    return jax.shard_map(
        on_device,
        mesh=mesh,
        in_specs=placed,
        out_specs=(P("section", ("dp", "tensor"), None), P("section", "dp", "tensor")),
        check_vma=False,
    )
```

profile of v0, /device:TPU:1, one launch (start us, length us, event | category | flops | bytes accessed | tf_op | source)
XLA Modules:
  0.0 710.5 jit_solution(3716013409856002741)
XLA Ops:
  7.2 2.5 copy.46
  9.6 6.6 all-to-all-start
  16.3 17.9 %all-to-all-done = bf16[128,4,1280]{2,0,1:T(8,128)(2,1)S(1)} async-done(((bf16[128,4,1280]{2,0,1:T(8,128)(2,1)}), bf16[128,4,1280]{2,0,1:T(8,128)(2,1)S(1)}, u32[]{:S(2)}, u32[]{:S(2)}) %all-to-all-start) | async-done | bytes 1310752 | tf_op jit(solution)/shard_map/all_to_all | solution.py:26
  34.2 1.1 copy-done.4
  35.2 3.0 conditional.4
  35.2 3.0 broadcast.8
  38.2 7.9 %copy.25 = bf16[512,5120]{0,1:T(8,128)(2,1)} copy(bf16[512,5120]{1,0:T(8,128)(2,1)} %get-tuple-element.46) | data formatting | bytes 10485760 | tf_op jit(solution)/shard_map/cond | solution.py:37
  46.2 7.9 %copy.34 = bf16[512,5120]{1,0:T(8,128)(2,1)} copy(bf16[512,5120]{0,1:T(8,128)(2,1)} %copy.25) | data formatting | bytes 10485760
  54.1 1.3 copy-done
  55.4 0.8 copy.23
  56.2 66.3 %reduce-scatter.16.cloned.1.call-done = bf16[128,5120]{1,0:T(8,128)(2,1)} async-done(((bf16[512,5120]{1,0:T(8,128)(2,1)}), bf16[128,5120]{1,0:T(8,128)(2,1)}) %reduce-scatter.16.cloned.1.call-update) | async-done | bytes 1310736
  122.5 1.8 copy.35
  124.2 0.3 add_convert_fusion.3
  124.6 1.3 collective-permute-start
  125.9 30.2 %collective-permute-done = bf16[128,5120]{0,1:T(8,128)(2,1)S(1)} collective-permute-done((bf16[128,5120]{0,1:T(8,128)(2,1)S(1)}, bf16[128,5120]{0,1:T(8,128)(2,1)S(1)}, u32[]{:S(2)}, u32[]{:S(2)}) %collective-permute-start) | collective-permute-done | bytes 1310752 | tf_op jit(solution)/shard_map/ppermute | solution.py:10
  156.1 1.4 copy.26
  157.6 5.1 all-to-all-start.1
  162.6 17.9 %all-to-all-done.1 = bf16[128,4,1280]{2,0,1:T(8,128)(2,1)S(1)} async-done(((bf16[128,4,1280]{2,0,1:T(8,128)(2,1)}), bf16[128,4,1280]{2,0,1:T(8,128)(2,1)S(1)}, u32[]{:S(2)}, u32[]{:S(2)}) %all-to-all-start.1) | async-done | bytes 1310752 | tf_op jit(solution)/shard_map/all_to_all | solution.py:26
  180.5 1.1 copy-done.6
  181.6 3.0 conditional.5
  181.6 3.0 broadcast.9
  184.6 7.9 %copy.27 = bf16[512,5120]{0,1:T(8,128)(2,1)} copy(bf16[512,5120]{1,0:T(8,128)(2,1)} %get-tuple-element.47) | data formatting | bytes 10485760 | tf_op jit(solution)/shard_map/cond | solution.py:37
  192.6 7.9 %copy.36 = bf16[512,5120]{1,0:T(8,128)(2,1)} copy(bf16[512,5120]{0,1:T(8,128)(2,1)} %copy.27) | data formatting | bytes 10485760
  200.4 68.0 %reduce-scatter.18.cloned.1.call-done = bf16[128,5120]{1,0:T(8,128)(2,1)} async-done(((bf16[512,5120]{1,0:T(8,128)(2,1)}), bf16[128,5120]{1,0:T(8,128)(2,1)}) %reduce-scatter.18.cloned.1.call-update) | async-done | bytes 1310736
  268.4 1.8 copy.37
  270.2 0.3 add_convert_fusion.2
  270.6 1.3 collective-permute-start.1
  271.9 30.2 %collective-permute-done.1 = bf16[128,5120]{0,1:T(8,128)(2,1)S(1)} collective-permute-done((bf16[128,5120]{0,1:T(8,128)(2,1)S(1)}, bf16[128,5120]{0,1:T(8,128)(2,1)S(1)}, u32[]{:S(2)}, u32[]{:S(2)}) %collective-permute-start.1) | collective-permute-done | bytes 1310752 | tf_op jit(solution)/shard_map/ppermute | solution.py:10
  302.1 1.4 copy.28
  303.5 5.1 all-to-all-start.2
  308.6 17.9 %all-to-all-done.2 = bf16[128,4,1280]{2,0,1:T(8,128)(2,1)S(1)} async-done(((bf16[128,4,1280]{2,0,1:T(8,128)(2,1)}), bf16[128,4,1280]{2,0,1:T(8,128)(2,1)S(1)}, u32[]{:S(2)}, u32[]{:S(2)}) %all-to-all-start.2) | async-done | bytes 1310752 | tf_op jit(solution)/shard_map/all_to_all | solution.py:26
  326.5 1.1 copy-done.7
  327.6 3.0 conditional.6
  327.6 3.0 broadcast.10
  330.6 7.9 %copy.29 = bf16[512,5120]{0,1:T(8,128)(2,1)} copy(bf16[512,5120]{1,0:T(8,128)(2,1)} %get-tuple-element.48) | data formatting | bytes 10485760 | tf_op jit(solution)/shard_map/cond | solution.py:37
  338.5 7.9 %copy.38 = bf16[512,5120]{1,0:T(8,128)(2,1)} copy(bf16[512,5120]{0,1:T(8,128)(2,1)} %copy.29) | data formatting | bytes 10485760
  346.4 0.0 all-gather.3.cloned.1.call-start
  346.5 0.5 all-gather.3.cloned.1.call-update
  347.0 65.9 %reduce-scatter.20.cloned.1.call-done = bf16[128,5120]{1,0:T(8,128)(2,1)} async-done(((bf16[512,5120]{1,0:T(8,128)(2,1)}), bf16[128,5120]{1,0:T(8,128)(2,1)}) %reduce-scatter.20.cloned.1.call-update) | async-done | bytes 1310736
  412.9 1.8 copy.39
  414.7 0.3 add_convert_fusion.1
  415.1 1.3 collective-permute-start.2
  416.4 30.3 %collective-permute-done.2 = bf16[128,5120]{0,1:T(8,128)(2,1)S(1)} collective-permute-done((bf16[128,5120]{0,1:T(8,128)(2,1)S(1)}, bf16[128,5120]{0,1:T(8,128)(2,1)S(1)}, u32[]{:S(2)}, u32[]{:S(2)}) %collective-permute-start.2) | collective-permute-done | bytes 1310752 | tf_op jit(solution)/shard_map/ppermute | solution.py:10
  446.7 1.4 copy.30
  448.1 5.0 all-to-all-start.3
  453.1 17.9 %all-to-all-done.3 = bf16[128,4,1280]{2,0,1:T(8,128)(2,1)S(1)} async-done(((bf16[128,4,1280]{2,0,1:T(8,128)(2,1)}), bf16[128,4,1280]{2,0,1:T(8,128)(2,1)S(1)}, u32[]{:S(2)}, u32[]{:S(2)}) %all-to-all-start.3) | async-done | bytes 1310752 | tf_op jit(solution)/shard_map/all_to_all | solution.py:26
  471.0 1.1 copy-done.8
  472.1 13.4 %conditional.7 = (bf16[512,5120]{1,0:T(8,128)(2,1)}) conditional(s32[]{:T(128)} %convert_element_type.83, () %tuple.38, (bf16[512,1280]{1,0:T(8,128)(2,1)S(1)}, bf16[5120,1280]{1,0:T(8,128)(2,1)}) %tuple.72), branch_computations={%region_9.10_spmd, %region_10.11_spmd} | conditional | flops 6710886400 | bytes 19660808 | solution.py:37
  472.1 13.4 %fusion.17 = bf16[512,5120]{1,0:T(8,128)(2,1)} fusion(bf16[512,1280]{1,0:T(8,128)(2,1)S(1)} %get-tuple-element.34, bf16[5120,1280]{1,0:T(8,128)(2,1)} %get-tuple-element.35), kind=kOutput, calls=%fused_computation.24 | convolution fusion | flops 6710886400 | bytes 19660800 | tf_op jit(solution)/shard_map/cond/branch_1_fun/dot_general | solution.py:29
  485.5 8.0 %copy.31 = bf16[512,5120]{0,1:T(8,128)(2,1)} copy(bf16[512,5120]{1,0:T(8,128)(2,1)} %get-tuple-element.49) | data formatting | bytes 10485760 | tf_op jit(solution)/shard_map/cond | solution.py:37
  493.4 8.0 %copy.40 = bf16[512,5120]{1,0:T(8,128)(2,1)} copy(bf16[512,5120]{0,1:T(8,128)(2,1)} %copy.31) | data formatting | bytes 10485760
  501.4 0.3 reduce-scatter.24.cloned.1.call-start
  501.7 0.0 all-gather.3.cloned.1.call-done
  501.7 1.0 copy-done.5
  502.7 12.3 %fusion = bf16[5120,1280]{0,1:T(8,128)(2,1)} fusion(bf16[1,512,5120]{2,1,0:T(8,128)(2,1)} %all-gather.3.cloned.1.call-done, bf16[512,1280]{1,0:T(8,128)(2,1)} %bitcast.54, bf16[512,1280]{1,0:T(8,128)(2,1)} %bitcast.52, bf16[512,1280]{1,0:T(8,128)(2,1)} %bitcast.50, bf16[512,1280]{1,0:T(8,128)(2,1)S(1)} %bitcast.48, pred[]{:T(512)S(6)} %eq.13, pred[]{:T(512)S(6)} %eq.14, ...), kind=kOutput, calls=%fused_computation.1 | convolution fusion | flops 6720061440 | bytes 23592964 | tf_op jit(solution)/shard_map/dot_general | solution.py:49
  515.0 17.9 %copy.42 = bf16[5120,1280]{1,0:T(8,128)(2,1)} copy(bf16[5120,1280]{0,1:T(8,128)(2,1)} %fusion) | data formatting | bytes 26214400
  532.9 23.7 %reduce-scatter.22.cloned.1.call-done = bf16[128,5120]{1,0:T(8,128)(2,1)} async-done(((bf16[512,5120]{1,0:T(8,128)(2,1)}), bf16[128,5120]{1,0:T(8,128)(2,1)}) %reduce-scatter.22.cloned.1.call-update) | async-done | bytes 1310736
  556.6 1.8 copy.41
  558.4 1.6 fusion.3
  559.9 2.4 copy.32
  562.4 133.1 %reduce-scatter.24.cloned.1.call-done = bf16[640,1280]{1,0:T(8,128)(2,1)} async-done(((bf16[5120,1280]{1,0:T(8,128)(2,1)}), bf16[640,1280]{1,0:T(8,128)(2,1)}) %reduce-scatter.24.cloned.1.call-update) | async-done | bytes 1638416
  695.5 3.5 copy.43
  699.0 1.6 bitcast_convert_fusion
  700.6 3.0 copy.33
  (21 shorter events, 0.1 us)
Async XLA Ops:
  9.6 24.6 %all-to-all-start = ((bf16[128,4,1280]{2,0,1:T(8,128)(2,1)}), bf16[128,4,1280]{2,0,1:T(8,128)(2,1)S(1)}, u32[]{:S(2)}, u32[]{:S(2)}) async-start(bf16[128,4,1280]{2,0,1:T(8,128)(2,1)} %bitcast.42), calls=%async_computation | async-start | bytes 2621440 | tf_op jit(solution)/shard_map/all_to_all | solution.py:26
  16.3 106.2 %reduce-scatter.16.cloned.1.call-start = ((), (), s32[]{:S(2)}) async-start(), calls=%async_computation.10 | async-start | bytes 6553600
  34.2 1.1 copy-start.4
  54.1 1.3 copy-start
  124.6 31.5 %copy-start.1 = (bf16[128,5120]{0,1:T(8,128)(2,1)}, bf16[128,5120]{0,1:T(8,128)(2,1)S(1)}, u32[]{:S(2)}) copy-start(bf16[128,5120]{0,1:T(8,128)(2,1)S(1)} %add_convert_fusion.3) | copy-start | bytes 3932164
  124.6 31.5 %collective-permute-start = (bf16[128,5120]{0,1:T(8,128)(2,1)S(1)}, bf16[128,5120]{0,1:T(8,128)(2,1)S(1)}, u32[]{:S(2)}, u32[]{:S(2)}) collective-permute-start(bf16[128,5120]{0,1:T(8,128)(2,1)S(1)} %add_convert_fusion.3), channel_id=1, source_target_pairs={{32,0},{64,32},{96,64},{33,1},{65,33},{97,65},{34,2},{66,34},{98,6... | collective-permute-start | bytes 3932168 | tf_op jit(solution)/shard_map/ppermute | solution.py:10
  157.6 23.0 %all-to-all-start.1 = ((bf16[128,4,1280]{2,0,1:T(8,128)(2,1)}), bf16[128,4,1280]{2,0,1:T(8,128)(2,1)S(1)}, u32[]{:S(2)}, u32[]{:S(2)}) async-start(bf16[128,4,1280]{2,0,1:T(8,128)(2,1)} %copy.26), calls=%async_computation.1 | async-start | bytes 2621440 | tf_op jit(solution)/shard_map/all_to_all | solution.py:26
  162.6 105.8 %reduce-scatter.18.cloned.1.call-start = ((), (), s32[]{:S(2)}) async-start(), calls=%async_computation.11 | async-start | bytes 6553600
  180.5 1.1 copy-start.6
  270.6 31.6 %copy-start.2 = (bf16[128,5120]{0,1:T(8,128)(2,1)}, bf16[128,5120]{0,1:T(8,128)(2,1)S(1)}, u32[]{:S(2)}) copy-start(bf16[128,5120]{0,1:T(8,128)(2,1)S(1)} %add_convert_fusion.2) | copy-start | bytes 3932164
  270.6 31.5 %collective-permute-start.1 = (bf16[128,5120]{0,1:T(8,128)(2,1)S(1)}, bf16[128,5120]{0,1:T(8,128)(2,1)S(1)}, u32[]{:S(2)}, u32[]{:S(2)}) collective-permute-start(bf16[128,5120]{0,1:T(8,128)(2,1)S(1)} %add_convert_fusion.2), channel_id=1, source_target_pairs={{32,0},{64,32},{96,64},{33,1},{65,33},{97,65},{34,2},{66,34},{98,6... | collective-permute-start | bytes 3932168 | tf_op jit(solution)/shard_map/ppermute | solution.py:10
  303.5 23.0 %all-to-all-start.2 = ((bf16[128,4,1280]{2,0,1:T(8,128)(2,1)}), bf16[128,4,1280]{2,0,1:T(8,128)(2,1)S(1)}, u32[]{:S(2)}, u32[]{:S(2)}) async-start(bf16[128,4,1280]{2,0,1:T(8,128)(2,1)} %copy.28), calls=%async_computation.2 | async-start | bytes 2621440 | tf_op jit(solution)/shard_map/all_to_all | solution.py:26
  308.6 104.3 %reduce-scatter.20.cloned.1.call-start = ((), (), s32[]{:S(2)}) async-start(), calls=%async_computation.12 | async-start | bytes 6553600
  326.5 1.1 copy-start.7
  346.4 155.3 %all-gather.3.cloned.1.call-start = ((), (), s32[]{:S(2)}) async-start(), calls=%async_computation.9 | async-start | bytes 6553600 | tf_op jit(solution)/shard_map/all_gather | solution.py:47
  415.1 31.7 %copy-start.3 = (bf16[128,5120]{0,1:T(8,128)(2,1)}, bf16[128,5120]{0,1:T(8,128)(2,1)S(1)}, u32[]{:S(2)}) copy-start(bf16[128,5120]{0,1:T(8,128)(2,1)S(1)} %add_convert_fusion.1) | copy-start | bytes 3932164
  415.1 31.6 %collective-permute-start.2 = (bf16[128,5120]{0,1:T(8,128)(2,1)S(1)}, bf16[128,5120]{0,1:T(8,128)(2,1)S(1)}, u32[]{:S(2)}, u32[]{:S(2)}) collective-permute-start(bf16[128,5120]{0,1:T(8,128)(2,1)S(1)} %add_convert_fusion.1), channel_id=1, source_target_pairs={{32,0},{64,32},{96,64},{33,1},{65,33},{97,65},{34,2},{66,34},{98,6... | collective-permute-start | bytes 3932168 | tf_op jit(solution)/shard_map/ppermute | solution.py:10
  448.1 22.9 %all-to-all-start.3 = ((bf16[128,4,1280]{2,0,1:T(8,128)(2,1)}), bf16[128,4,1280]{2,0,1:T(8,128)(2,1)S(1)}, u32[]{:S(2)}, u32[]{:S(2)}) async-start(bf16[128,4,1280]{2,0,1:T(8,128)(2,1)} %copy.30), calls=%async_computation.3 | async-start | bytes 2621440 | tf_op jit(solution)/shard_map/all_to_all | solution.py:26
  453.1 103.5 %reduce-scatter.22.cloned.1.call-start = ((), (), s32[]{:S(2)}) async-start(), calls=%async_computation.13 | async-start | bytes 6553600
  471.0 1.1 copy-start.8
  501.4 1.3 copy-start.5
  501.4 194.1 %reduce-scatter.24.cloned.1.call-start = ((), (), s32[]{:S(2)}) async-start(), calls=%async_computation.14 | async-start | bytes 14745600
Sparse Core Ops, SparseCore 0:
  54.2 68.1 reduce-scatter.15
  200.6 67.8 reduce-scatter.17
  346.5 66.3 reduce-scatter.19
  414.6 44.2 all-gather.2
  501.5 55.0 reduce-scatter.21
  558.9 136.5 reduce-scatter.23
where the time goes:
time: 713 us; the launch traced here: 710 us
  waiting for transfers between devices  520 us (73%)
  local copies, waits for them, and re-layouts  120 us (17%)
  starting transfers between devices  25.9 us (4%)
  matrix products  25.7 us (4%)
  between operations  14.2 us (2%)
    unnamed x11, waiting for transfers between devices  358 us
    ppermute x3, waiting for transfers between devices, from_behind(): return lax.ppermute(block, axis, route)  90.8 us
    unnamed x31, local copies, waits for them, and re-layouts  72.7 us
    all_to_all x4, waiting for transfers between devices, on_device(): lax.all_to_all(gradient, 'tensor', split_axis=1, concat_axis=0, tiled=True)  71.6 us
    cond x4, local copies, waits for them, and re-layouts, on_device(): lax.cond(on_duty, compute, nothing, columns).astype(jnp.bfloat16)  31.8 us
    all_to_all x4, starting transfers between devices, on_device(): lax.all_to_all(gradient, 'tensor', split_axis=1, concat_axis=0, tiled=True)  21.7 us
  transfers between devices with their start and end apart: 13, of which 12 were waited for; matrix products, arithmetic and copies ran while one was open for 10% of the time, Pallas kernels for 0%

commit v1 on v0

--- a/solution.py
+++ b/solution.py
@@ -23,7 +23,10 @@
     for rounds in range(sections):
         active = sections - 1 - rounds
         on_duty = section_index == active
-        columns = lax.all_to_all(gradient, "tensor", split_axis=1, concat_axis=0, tiled=True)
+        z1 = lax.all_to_all(
+            jnp.stack(jnp.split(gradient, lax.psum(1, "tensor"), 1), 0), "tensor", 0, 0
+        )
+        columns = jnp.concatenate(z1, 0)
 
         def compute(operand):
             return lax.dot_general(

time: 713 us -> 646 us (0.906)
  local copies, waits for them, and re-layouts: 120 us -> 35.9 us
  other arithmetic: 4.22 us -> 14.2 us
    reduce_scatter x0 -> x4, waiting for transfers between devices: none -> 228 us  [on_device(): lax.psum_scatter(lax.cond(on_duty, compute, nothing, columns).astype(jnp....]
    unnamed x11 -> x7, waiting for transfers between devices: 358 us -> 136 us
    unnamed x31 -> x11, local copies, waits for them, and re-layouts: 72.7 us -> 25.4 us
    cond x4 -> x0, local copies, waits for them, and re-layouts: 31.8 us -> none  [on_device(): lax.cond(on_duty, compute, nothing, columns).astype(jnp.bfloat16)]
  transfers between devices with their start and end apart: 13 -> 13, of which waited for: 12 -> 12; matrix products, arithmetic and copies ran while one was open for 10% -> 8% of each run, Pallas kernels for 0% -> 0%
where the time goes in v1:
time: 646 us; the launch traced here: 645 us
  waiting for transfers between devices  527 us (82%)
  local copies, waits for them, and re-layouts  35.9 us (6%)
  starting transfers between devices  28.1 us (4%)
  matrix products  26 us (4%)
  other arithmetic  14.2 us (2%)
  between operations  14.2 us (2%)
    reduce_scatter x4, waiting for transfers between devices, on_device(): lax.psum_scatter(lax.cond(on_duty, compute, nothing, columns).astype(jnp....  228 us
    unnamed x7, waiting for transfers between devices  136 us
    ppermute x3, waiting for transfers between devices, from_behind(): return lax.ppermute(block, axis, route)  90.8 us
    all_to_all x4, waiting for transfers between devices, on_device(): lax.all_to_all(jnp.stack(jnp.split(gradient, lax.psum(1, 'tensor'), 1), 0...  71.9 us
    unnamed x11, local copies, waits for them, and re-layouts  25.4 us
    all_to_all x4, starting transfers between devices, on_device(): lax.all_to_all(jnp.stack(jnp.split(gradient, lax.psum(1, 'tensor'), 1), 0...  23.9 us
    dot_general x1, matrix products, compute(): lax.dot_general(operand, weight_cols, (((1,), (1,)), ((), ())), preferred...  13.6 us
  transfers between devices with their start and end apart: 13, of which 12 were waited for; matrix products, arithmetic and copies ran while one was open for 8% of the time, Pallas kernels for 0%

profile of v1, /device:TPU:1, one launch (start us, length us, event | category | flops | bytes accessed | tf_op | source)
XLA Modules:
  0.0 645.3 jit_solution(10064587181311850208)
XLA Ops:
  7.2 1.4 slice_bitcast_fusion.15
  8.5 1.2 pad_maximum_fusion
  9.8 6.6 %all-to-all-start = ((bf16[4,128,1280]{2,1,0:T(8,128)(2,1)}), bf16[4,128,1280]{2,1,0:T(8,128)(2,1)S(1)}, u32[]{:S(2)}, u32[]{:S(2)}) async-start(bf16[4,128,1280]{2,1,0:T(8,128)(2,1)} %pad_maximum_fusion), calls=%async_computation | async-start | bytes 2621440 | tf_op jit(solution)/shard_map/all_to_all | solution.py:26
  16.4 0.0 reduce-scatter.8.cloned.1.call-start
  16.4 17.9 %all-to-all-done = bf16[4,128,1280]{2,1,0:T(8,128)(2,1)S(1)} async-done(((bf16[4,128,1280]{2,1,0:T(8,128)(2,1)}), bf16[4,128,1280]{2,1,0:T(8,128)(2,1)S(1)}, u32[]{:S(2)}, u32[]{:S(2)}) %all-to-all-start) | async-done | bytes 1310752 | tf_op jit(solution)/shard_map/all_to_all | solution.py:26
  34.3 0.0 copy-start.3
  34.3 1.1 copy-done.3
  35.4 3.0 conditional.4
  35.4 3.0 broadcast.8
  38.3 0.0 reduce-scatter.8.cloned.1.call-update
  38.4 68.4 %reduce-scatter.8.cloned.1.call-done = bf16[128,5120]{1,0:T(8,128)(2,1)} async-done(((bf16[512,5120]{1,0:T(8,128)(2,1)}), bf16[128,5120]{1,0:T(8,128)(2,1)}) %reduce-scatter.8.cloned.1.call-update) | async-done | bytes 1310736 | tf_op jit(solution)/shard_map/reduce_scatter | solution.py:39
  106.8 0.0 copy-done
  106.8 1.6 add_convert_fusion.3
  108.4 1.3 collective-permute-start
  109.7 30.3 %collective-permute-done = bf16[128,5120]{1,0:T(8,128)(2,1)S(1)} collective-permute-done((bf16[128,5120]{1,0:T(8,128)(2,1)S(1)}, bf16[128,5120]{1,0:T(8,128)(2,1)S(1)}, u32[]{:S(2)}, u32[]{:S(2)}) %collective-permute-start) | collective-permute-done | bytes 1310752 | tf_op jit(solution)/shard_map/ppermute | solution.py:10
  140.0 0.1 slice_bitcast_fusion.11
  140.0 1.2 pad_maximum_fusion.1
  141.3 5.8 all-to-all-start.1
  147.0 0.0 reduce-scatter.10.cloned.1.call-start
  147.0 18.0 %all-to-all-done.1 = bf16[4,128,1280]{2,1,0:T(8,128)(2,1)} async-done(((bf16[4,128,1280]{2,1,0:T(8,128)(2,1)}), bf16[4,128,1280]{2,1,0:T(8,128)(2,1)}, u32[]{:S(2)}, u32[]{:S(2)}) %all-to-all-start.1) | async-done | bytes 1310752 | tf_op jit(solution)/shard_map/all_to_all | solution.py:26
  165.1 3.0 conditional.5
  165.1 3.0 broadcast.9
  168.0 0.0 reduce-scatter.10.cloned.1.call-update
  168.0 68.2 %reduce-scatter.10.cloned.1.call-done = bf16[128,5120]{1,0:T(8,128)(2,1)} async-done(((bf16[512,5120]{1,0:T(8,128)(2,1)}), bf16[128,5120]{1,0:T(8,128)(2,1)}) %reduce-scatter.10.cloned.1.call-update) | async-done | bytes 1310736 | tf_op jit(solution)/shard_map/reduce_scatter | solution.py:39
  236.3 1.6 add_convert_fusion.2
  237.9 0.0 copy-start.1
  237.9 1.3 collective-permute-start.1
  239.2 30.2 %collective-permute-done.1 = bf16[128,5120]{1,0:T(8,128)(2,1)S(1)} collective-permute-done((bf16[128,5120]{1,0:T(8,128)(2,1)S(1)}, bf16[128,5120]{1,0:T(8,128)(2,1)S(1)}, u32[]{:S(2)}, u32[]{:S(2)}) %collective-permute-start.1) | collective-permute-done | bytes 1310752 | tf_op jit(solution)/shard_map/ppermute | solution.py:10
  269.5 0.1 slice_bitcast_fusion.7
  269.5 0.0 copy-done.1
  269.6 1.2 pad_maximum_fusion.2
  270.8 5.8 all-to-all-start.2
  276.6 0.0 reduce-scatter.12.cloned.1.call-start
  276.6 18.0 %all-to-all-done.2 = bf16[4,128,1280]{2,1,0:T(8,128)(2,1)} async-done(((bf16[4,128,1280]{2,1,0:T(8,128)(2,1)}), bf16[4,128,1280]{2,1,0:T(8,128)(2,1)}, u32[]{:S(2)}, u32[]{:S(2)}) %all-to-all-start.2) | async-done | bytes 1310752 | tf_op jit(solution)/shard_map/all_to_all | solution.py:26
  294.6 3.0 conditional.6
  294.6 3.0 broadcast.10
  297.6 0.0 reduce-scatter.12.cloned.1.call-update
  297.6 0.2 all-gather.3.cloned.1.call-start
  297.8 0.3 all-gather.3.cloned.1.call-update
  298.2 66.2 %reduce-scatter.12.cloned.1.call-done = bf16[128,5120]{1,0:T(8,128)(2,1)} async-done(((bf16[512,5120]{1,0:T(8,128)(2,1)}), bf16[128,5120]{1,0:T(8,128)(2,1)}) %reduce-scatter.12.cloned.1.call-update) | async-done | bytes 1310736 | tf_op jit(solution)/shard_map/reduce_scatter | solution.py:39
  364.4 1.6 add_convert_fusion.1
  366.0 0.0 copy-start.2
  366.0 1.3 collective-permute-start.2
  367.3 30.3 %collective-permute-done.2 = bf16[128,5120]{1,0:T(8,128)(2,1)S(1)} collective-permute-done((bf16[128,5120]{1,0:T(8,128)(2,1)S(1)}, bf16[128,5120]{1,0:T(8,128)(2,1)S(1)}, u32[]{:S(2)}, u32[]{:S(2)}) %collective-permute-start.2) | collective-permute-done | bytes 1310752 | tf_op jit(solution)/shard_map/ppermute | solution.py:10
  397.6 0.1 slice_bitcast_fusion.3
  397.7 0.0 copy-done.2
  397.7 1.2 pad_maximum_fusion.3
  399.0 5.7 all-to-all-start.3
  404.7 0.0 reduce-scatter.14.cloned.1.call-start
  404.7 18.0 %all-to-all-done.3 = bf16[4,128,1280]{2,1,0:T(8,128)(2,1)} async-done(((bf16[4,128,1280]{2,1,0:T(8,128)(2,1)}), bf16[4,128,1280]{2,1,0:T(8,128)(2,1)}, u32[]{:S(2)}, u32[]{:S(2)}) %all-to-all-start.3) | async-done | bytes 1310752 | tf_op jit(solution)/shard_map/all_to_all | solution.py:26
  422.7 13.6 %conditional.7 = (bf16[512,5120]{1,0:T(8,128)(2,1)}) conditional(s32[]{:T(128)} %convert_element_type.83, () %tuple.38, (bf16[512,1280]{1,0:T(8,128)(2,1)}, bf16[5120,1280]{1,0:T(8,128)(2,1)}) %tuple.79), branch_computations={%region_9.10_spmd, %region_10.11_spmd} | conditional | flops 6710886400 | bytes 19660808 | solution.py:40
  422.7 13.6 %fusion.17 = bf16[512,5120]{1,0:T(8,128)(2,1)} fusion(bf16[512,1280]{1,0:T(8,128)(2,1)} %get-tuple-element.34, bf16[5120,1280]{1,0:T(8,128)(2,1)} %get-tuple-element.35), kind=kOutput, calls=%fused_computation.43 | convolution fusion | flops 6710886400 | bytes 19660800 | tf_op jit(solution)/shard_map/cond/branch_1_fun/dot_general | solution.py:32
  436.3 0.0 reduce-scatter.14.cloned.1.call-update
  436.3 0.0 reduce-scatter.16.cloned.1.call-start
  436.4 0.0 all-gather.3.cloned.1.call-done
  436.4 12.4 %fusion = bf16[5120,1280]{0,1:T(8,128)(2,1)} fusion(bf16[1,512,5120]{2,1,0:T(8,128)(2,1)} %all-gather.3.cloned.1.call-done, bf16[512,1280]{1,0:T(8,128)(2,1)} %bitcast.20, bf16[512,1280]{1,0:T(8,128)(2,1)} %bitcast.15, bf16[512,1280]{1,0:T(8,128)(2,1)} %bitcast.10, bf16[512,1280]{1,0:T(8,128)(2,1)} %bitcast.57, pred[]{:T(512)S(6)} %eq.13, pred[]{:T(512)S(6)} %eq.14, ...), kind=kOutput, calls=%fused_computation.1 | convolution fusion | flops 6720061440 | bytes 23592964 | tf_op jit(solution)/shard_map/dot_general | solution.py:52
  448.8 17.8 %copy.7 = bf16[5120,1280]{1,0:T(8,128)(2,1)} copy(bf16[5120,1280]{0,1:T(8,128)(2,1)} %fusion) | data formatting | bytes 26214400
  466.6 0.0 reduce-scatter.16.cloned.1.call-update
  466.6 24.8 %reduce-scatter.14.cloned.1.call-done = bf16[128,5120]{1,0:T(8,128)(2,1)} async-done(((bf16[512,5120]{1,0:T(8,128)(2,1)}), bf16[128,5120]{1,0:T(8,128)(2,1)}) %reduce-scatter.14.cloned.1.call-update) | async-done | bytes 1310736 | tf_op jit(solution)/shard_map/reduce_scatter | solution.py:39
  491.4 2.8 fusion.3
  494.3 136.0 %reduce-scatter.16.cloned.1.call-done = bf16[640,1280]{1,0:T(8,128)(2,1)} async-done(((bf16[5120,1280]{1,0:T(8,128)(2,1)}), bf16[640,1280]{1,0:T(8,128)(2,1)}) %reduce-scatter.16.cloned.1.call-update) | async-done | bytes 1638416
  630.3 3.5 copy.8
  633.8 1.6 bitcast_convert_fusion
  635.5 3.0 copy.6
  (1 shorter events, 0.0 us)
Async XLA Ops:
  9.8 24.6 %all-to-all-start = ((bf16[4,128,1280]{2,1,0:T(8,128)(2,1)}), bf16[4,128,1280]{2,1,0:T(8,128)(2,1)S(1)}, u32[]{:S(2)}, u32[]{:S(2)}) async-start(bf16[4,128,1280]{2,1,0:T(8,128)(2,1)} %pad_maximum_fusion), calls=%async_computation | async-start | bytes 2621440 | tf_op jit(solution)/shard_map/all_to_all | solution.py:26
  16.4 90.4 %reduce-scatter.8.cloned.1.call-start = ((), (), s32[]{:S(2)}) async-start(), calls=%async_computation.9 | async-start | bytes 6553600 | tf_op jit(solution)/shard_map/reduce_scatter | solution.py:39
  34.3 1.1 copy-start.3
  38.3 68.4 %copy-start = (bf16[128,5120]{1,0:T(8,128)(2,1)S(1)}, bf16[128,5120]{1,0:T(8,128)(2,1)}, u32[]{:S(2)}) copy-start(bf16[128,5120]{1,0:T(8,128)(2,1)} %param.13) | copy-start | bytes 3932164
  108.4 31.6 %collective-permute-start = (bf16[128,5120]{1,0:T(8,128)(2,1)S(1)}, bf16[128,5120]{1,0:T(8,128)(2,1)S(1)}, u32[]{:S(2)}, u32[]{:S(2)}) collective-permute-start(bf16[128,5120]{1,0:T(8,128)(2,1)S(1)} %add_convert_fusion.3), channel_id=1, source_target_pairs={{32,0},{64,32},{96,64},{33,1},{65,33},{97,65},{34,2},{66,34},{98,6... | collective-permute-start | bytes 3932168 | tf_op jit(solution)/shard_map/ppermute | solution.py:10
  141.3 23.8 %all-to-all-start.1 = ((bf16[4,128,1280]{2,1,0:T(8,128)(2,1)}), bf16[4,128,1280]{2,1,0:T(8,128)(2,1)}, u32[]{:S(2)}, u32[]{:S(2)}) async-start(bf16[4,128,1280]{2,1,0:T(8,128)(2,1)} %pad_maximum_fusion.1), calls=%async_computation.2 | async-start | bytes 2621440 | tf_op jit(solution)/shard_map/all_to_all | solution.py:26
  147.0 89.2 %reduce-scatter.10.cloned.1.call-start = ((), (), s32[]{:S(2)}) async-start(), calls=%async_computation.10 | async-start | bytes 6553600 | tf_op jit(solution)/shard_map/reduce_scatter | solution.py:39
  237.9 31.6 %copy-start.1 = (bf16[128,5120]{1,0:T(8,128)(2,1)}, bf16[128,5120]{1,0:T(8,128)(2,1)S(1)}, u32[]{:S(2)}) copy-start(bf16[128,5120]{1,0:T(8,128)(2,1)S(1)} %add_convert_fusion.2) | copy-start | bytes 3932164
  237.9 31.5 %collective-permute-start.1 = (bf16[128,5120]{1,0:T(8,128)(2,1)S(1)}, bf16[128,5120]{1,0:T(8,128)(2,1)S(1)}, u32[]{:S(2)}, u32[]{:S(2)}) collective-permute-start(bf16[128,5120]{1,0:T(8,128)(2,1)S(1)} %add_convert_fusion.2), channel_id=1, source_target_pairs={{32,0},{64,32},{96,64},{33,1},{65,33},{97,65},{34,2},{66,34},{98,6... | collective-permute-start | bytes 3932168 | tf_op jit(solution)/shard_map/ppermute | solution.py:10
  270.8 23.8 %all-to-all-start.2 = ((bf16[4,128,1280]{2,1,0:T(8,128)(2,1)}), bf16[4,128,1280]{2,1,0:T(8,128)(2,1)}, u32[]{:S(2)}, u32[]{:S(2)}) async-start(bf16[4,128,1280]{2,1,0:T(8,128)(2,1)} %pad_maximum_fusion.2), calls=%async_computation.4 | async-start | bytes 2621440 | tf_op jit(solution)/shard_map/all_to_all | solution.py:26
  276.6 87.8 %reduce-scatter.12.cloned.1.call-start = ((), (), s32[]{:S(2)}) async-start(), calls=%async_computation.11 | async-start | bytes 6553600 | tf_op jit(solution)/shard_map/reduce_scatter | solution.py:39
  297.6 138.8 %all-gather.3.cloned.1.call-start = ((), (), s32[]{:S(2)}) async-start(), calls=%async_computation.13 | async-start | bytes 6553600 | tf_op jit(solution)/shard_map/all_gather | solution.py:50
  366.0 31.7 %copy-start.2 = (bf16[128,5120]{1,0:T(8,128)(2,1)}, bf16[128,5120]{1,0:T(8,128)(2,1)S(1)}, u32[]{:S(2)}) copy-start(bf16[128,5120]{1,0:T(8,128)(2,1)S(1)} %add_convert_fusion.1) | copy-start | bytes 3932164
  366.0 31.6 %collective-permute-start.2 = (bf16[128,5120]{1,0:T(8,128)(2,1)S(1)}, bf16[128,5120]{1,0:T(8,128)(2,1)S(1)}, u32[]{:S(2)}, u32[]{:S(2)}) collective-permute-start(bf16[128,5120]{1,0:T(8,128)(2,1)S(1)} %add_convert_fusion.1), channel_id=1, source_target_pairs={{32,0},{64,32},{96,64},{33,1},{65,33},{97,65},{34,2},{66,34},{98,6... | collective-permute-start | bytes 3932168 | tf_op jit(solution)/shard_map/ppermute | solution.py:10
  399.0 23.7 %all-to-all-start.3 = ((bf16[4,128,1280]{2,1,0:T(8,128)(2,1)}), bf16[4,128,1280]{2,1,0:T(8,128)(2,1)}, u32[]{:S(2)}, u32[]{:S(2)}) async-start(bf16[4,128,1280]{2,1,0:T(8,128)(2,1)} %pad_maximum_fusion.3), calls=%async_computation.6 | async-start | bytes 2621440 | tf_op jit(solution)/shard_map/all_to_all | solution.py:26
  404.7 86.8 %reduce-scatter.14.cloned.1.call-start = ((), (), s32[]{:S(2)}) async-start(), calls=%async_computation.12 | async-start | bytes 6553600 | tf_op jit(solution)/shard_map/reduce_scatter | solution.py:39
  436.3 194.0 %reduce-scatter.16.cloned.1.call-start = ((), (), s32[]{:S(2)}) async-start(), calls=%async_computation.14 | async-start | bytes 14745600
Sparse Core Ops, SparseCore 0:
  38.5 68.2 reduce-scatter.7
  168.2 68.0 reduce-scatter.9
  297.7 66.6 reduce-scatter.11
  366.0 44.2 all-gather.2
  436.4 54.9 reduce-scatter.13
  493.7 136.5 reduce-scatter.15
